TPU v7x, 32 devices: a whole 2x2x4 slice. The times are simulated.
32 devices in a mesh: space: 4 (over x, core), tm: 8 (over z, y).
Axes of the slice: x: 2, y: 2, z: 4, core: 2. Of those that a mesh axis runs over, the one named last changes fastest.
Arguments:
- snapshots: bfloat16 [4096, 65536], P('tm', 'space'), may hold values from -24 to 24
- freq_bins: int32 [2], replicated, may hold values from 1 to 127
Outputs:
- gram_matrix: float32 [2, 64, 64], replicated
- whitened: float32 [2, 64, 65536], P(None, None, ('space', 'tm'))
All inputs are finite; a program needn't handle non-finite values.
Results may differ from a plain program's by a relative error of at most 0.0041.
Values may be sent and summed in bfloat16 or wider, within the bound.
No kernel may reach another device: no remote copies, remote signals or barrier semaphores. Data moves between devices by JAX's collectives and lax.ppermute only.
A program may use at most 128 MiB of HBM per device.

v0:
```python
import jax
import jax.numpy as jnp
from jax import lax
from jax.sharding import PartitionSpec as P

NFFT = 256
HOP = 128
NF = 2
ridge_term = 0.01


def passed_along(array, axis, by):
    devices = lax.axis_size(axis)
    return lax.ppermute(array, axis, [(i, (i + by) % devices) for i in range(devices)])


def make_table(freq_bins):
    sample = jnp.arange(NFFT, dtype=jnp.int32)
    sample_f = sample.astype(jnp.float32)
    hann_taper = 0.5 - 0.5 * jnp.cos(2.0 * jnp.pi * sample_f / NFFT)
    window = hann_taper / jnp.sqrt(jnp.sum(hann_taper * hann_taper))
    phase_idx = freq_bins[:, None] * sample[None, :] % NFFT
    angles = 2.0 * jnp.pi * phase_idx.astype(jnp.float32) / NFFT
    table = jnp.stack([window * jnp.cos(angles), -window * jnp.sin(angles)], axis=1)
    return table.astype(jnp.bfloat16)


def on_device(snapshots, freq_bins):
    points = snapshots.shape[1]
    block_count = snapshots.shape[0] // HOP
    table_rows = make_table(freq_bins).reshape(NF * 2, NFFT)
    first_table = table_rows[:, :HOP]
    second_table = table_rows[:, HOP:]
    halves = snapshots.reshape(block_count, HOP, points)
    lead_part = jnp.einsum("ct,htp->chp", first_table, halves, preferred_element_type=jnp.float32)
    trail_part = jnp.einsum("ct,htp->chp", second_table, halves, preferred_element_type=jnp.float32)
    incoming = passed_along(trail_part[:, :1], "tm", -1)
    trail_own = trail_part[:, 1:]
    coeffs = lead_part + jnp.concatenate([trail_own, incoming], axis=1)
    slice_width = points // lax.axis_size("tm")
    position = lax.axis_index("tm") * slice_width
    local_cols = lax.dynamic_slice_in_dim(
        lax.all_gather(coeffs, "tm", axis=1, tiled=True), position, slice_width, 2
    )
    all_blocks_count = local_cols.shape[1]
    columns = local_cols.reshape(NF, 2 * all_blocks_count, slice_width)
    grid_total = points * lax.axis_size("space")
    partial_value = (
        jnp.einsum("fcp,fdp->fcd", columns, columns, precision=lax.Precision.HIGHEST) / grid_total
    )
    gram_matrix = lax.psum(partial_value, ("space", "tm"))
    identity = jnp.eye(2 * all_blocks_count, dtype=jnp.float32)
    factor = jnp.linalg.cholesky(gram_matrix + ridge_term * identity[None])
    whitened = lax.linalg.triangular_solve(factor, columns, left_side=True, lower=True)
    return (gram_matrix, whitened)


def solution(mesh):
    placed = (P("tm", "space"), P())
    return jax.shard_map(
        on_device,
        mesh=mesh,
        in_specs=placed,
        out_specs=(P(), P(None, None, ("space", "tm"))),
        check_vma=False,
    )
```

profile of v0, /device:TPU:0, one launch (start us, length us, event | category | flops | bytes accessed | tf_op | source)
XLA Modules:
  0.0 232.3 jit_solution(7412217076847700622)
XLA Ops:
  7.2 0.0 all-gather.2.cloned.1.call-start
  7.2 0.6 multiply_reduce_fusion
  8.6 0.8 multiply_convert_fusion.1
  9.4 0.0 copy-start
  9.4 8.2 %fusion.6 = f32[4,4,16384]{2,0,1:T(4,128)S(1)} fusion(bf16[4,128,16384]{2,1,0:T(8,128)(2,1)} %bitcast.24, bf16[4,256]{1,0:T(4,128)(2,1)S(1)} %convert_element_type.35), kind=kOutput, calls=%fused_computation.23 | convolution fusion | flops 67108864 | bytes 17826816 | tf_op jit(solution)/shard_map/ct,htp->chp/dot_general | solution.py:36
  17.7 6.1 %collective-permute-start = (f32[4,1,16384]{2,0,1:T(4,128)S(1)}, f32[4,1,16384]{2,0,1:T(4,128)S(1)}, u32[]{:S(2)}, u32[]{:S(2)}) collective-permute-start(f32[4,1,16384]{2,0,1:T(4,128)S(1)} %slice.29), channel_id=1, source_target_pairs={{0,7},{1,0},{2,1},{3,2},{4,3},{5,4},{6,5},{7,6},{8,15},{9,8},{10,9... | collective-permute-start | bytes 786440 | tf_op jit(solution)/shard_map/ppermute | solution.py:14
  23.7 0.1 slice.28
  23.8 5.5 %collective-permute-done = f32[4,1,16384]{2,0,1:T(4,128)S(1)} collective-permute-done((f32[4,1,16384]{2,0,1:T(4,128)S(1)}, f32[4,1,16384]{2,0,1:T(4,128)S(1)}, u32[]{:S(2)}, u32[]{:S(2)}) %collective-permute-start) | collective-permute-done | bytes 262176 | tf_op jit(solution)/shard_map/ppermute | solution.py:14
  29.3 0.0 copy-done
  29.3 3.3 %maximum_add_fusion = f32[4,4,16384]{2,0,1:T(4,128)} fusion(f32[4,1,16384]{2,0,1:T(4,128)S(1)} %collective-permute-done, f32[4,3,16384]{2,0,1:T(4,128)S(1)} %slice.28, bf16[4,128,16384]{2,1,0:T(8,128)(2,1)S(1)} %bitcast.25, bf16[4,256]{1,0:T(4,128)(2,1)S(1)} %convert_element_type.35), kind=kOutput, calls=%fused_computation.1 | convolution fusion | flops 67633152 | bytes 18875392 | tf_op jit(solution)/shard_map/ct,htp->chp/dot_general | solution.py:35
  32.6 0.0 all-gather.2.cloned.1.call-update
  32.6 0.1 copy.36
  32.7 126.4 %all-gather.2.cloned.1.call-done = f32[4,32,16384]{2,0,1:T(4,128)} async-done(((f32[4,4,16384]{2,0,1:T(4,128)}), f32[4,32,16384]{2,0,1:T(4,128)}) %all-gather.2.cloned.1.call-update) | async-done | bytes 8388624 | tf_op jit(solution)/shard_map/all_gather | solution.py:43
  159.1 1.3 constant_dynamic-slice_fusion
  160.4 0.6 copy.42
  161.0 1.1 convolution_multiply_fusion
  162.1 38.7 %psum.7 = f32[2,64,64]{1,2,0:T(8,128)S(1)} all-reduce(f32[2,64,64]{1,2,0:T(8,128)S(1)} %convolution_multiply_fusion), channel_id=1, replica_groups=mesh['space'=4,'tm'=8] {'space','tm'}, use_global_device_ids=true, to_apply=%region_1.2 | all-reduce | flops 8192 | bytes 65536 | tf_op jit(solution)/shard_map/psum | solution.py:51
  200.8 0.7 copy.39
  201.5 0.1 copy.37
  201.6 11.7 %custom-call.7 = f32[2,64,64]{2,1,0:T(8,128)S(1)} custom-call(f32[2,64,64]{2,1,0:T(8,128)S(1)} %fusion.2), custom_call_target="Cholesky" | custom-call | tf_op jit(solution)/shard_map/jit(cholesky)/cholesky | solution.py:53
  213.4 0.1 compare_reduce_fusion
  213.5 0.1 select_bitcast_fusion
  213.6 9.8 %custom-call.8 = f32[2,1,64,64]{2,3,1,0:T(8,128)S(1)} custom-call(f32[2,1,64,64]{3,2,1,0:T(8,128)S(1)} %select_bitcast_fusion), custom_call_target="InvertDiagBlocksLowerTriangular" | custom-call | tf_op jit(solution)/shard_map/triangular_solve | solution.py:54
  223.4 2.0 fusion
  (11 shorter events, 0.2 us)
Async XLA Ops:
  7.2 151.9 %all-gather.2.cloned.1.call-start = ((), (), s32[]{:S(2)}) async-start(), calls=%async_computation | async-start | bytes 9437184 | tf_op jit(solution)/shard_map/all_gather | solution.py:43
  9.4 19.9 %copy-start = (bf16[512,16384]{1,0:T(8,128)(2,1)S(1)}, bf16[512,16384]{1,0:T(8,128)(2,1)}, u32[]{:S(2)}) copy-start(bf16[512,16384]{1,0:T(8,128)(2,1)} %param.2) | copy-start | bytes 50331652
  17.7 11.7 %collective-permute-start = (f32[4,1,16384]{2,0,1:T(4,128)S(1)}, f32[4,1,16384]{2,0,1:T(4,128)S(1)}, u32[]{:S(2)}, u32[]{:S(2)}) collective-permute-start(f32[4,1,16384]{2,0,1:T(4,128)S(1)} %slice.29), channel_id=1, source_target_pairs={{0,7},{1,0},{2,1},{3,2},{4,3},{5,4},{6,5},{7,6},{8,15},{9,8},{10,9... | collective-permute-start | bytes 786440 | tf_op jit(solution)/shard_map/ppermute | solution.py:14
Sparse Core Ops, SparseCore 0:
  32.7 126.3 all-gather.1
where the time goes:
time: 233 us; the launch traced here: 232 us
  waiting for transfers between devices  132 us (57%)
  blocking collectives  38.7 us (17%)
  other arithmetic  23.3 us (10%)
  between operations  14.8 us (6%)
  matrix products  14.6 us (6%)
  starting transfers between devices  6.12 us (3%)
  local copies, waits for them, and re-layouts  2.87 us (1%)
    all_gather x1, waiting for transfers between devices, on_device(): lax.all_gather(coeffs, 'tm', axis=1, tiled=True)  126 us
    psum x1, blocking collectives, on_device(): gram_matrix = lax.psum(partial_value, ('space', 'tm'))  38.7 us
    another operation x4, other arithmetic, on_device(): factor = jnp.linalg.cholesky(gram_matrix + ridge_term * identity[None])  11.9 us
    another operation x3, other arithmetic, on_device(): lax.linalg.triangular_solve(factor, columns, left_side=True, lower=True)  9.92 us
    dot_general x1, matrix products, on_device(): jnp.einsum('ct,htp->chp', second_table, halves, preferred_element_type=jn...  8.19 us
    ppermute x1, starting transfers between devices, passed_along(): lax.ppermute(array, axis, [(i, (i + by) % devices) for i in range(devices)])  6.09 us
    ppermute x1, waiting for transfers between devices, passed_along(): lax.ppermute(array, axis, [(i, (i + by) % devices) for i in range(devices)])  5.51 us
  transfers between devices with their start and end apart: 2, of which 2 were waited for; matrix products, arithmetic and copies ran while one was open for 0% of the time, Pallas kernels for 0%

commit v1 on v0

--- a/solution.py
+++ b/solution.py
@@ -48,7 +48,7 @@
     partial_value = (
         jnp.einsum("fcp,fdp->fcd", columns, columns, precision=lax.Precision.HIGHEST) / grid_total
     )
-    gram_matrix = lax.psum(partial_value, ("space", "tm"))
+    gram_matrix = jnp.sum(lax.all_gather(partial_value, ("space", "tm")), axis=0)
     identity = jnp.eye(2 * all_blocks_count, dtype=jnp.float32)
     factor = jnp.linalg.cholesky(gram_matrix + ridge_term * identity[None])
     whitened = lax.linalg.triangular_solve(factor, columns, left_side=True, lower=True)

time: 233 us -> 250 us (1.073)
  waiting for transfers between devices: 132 us -> 187 us
  blocking collectives: 38.7 us -> 0 us
    all_gather x0 -> x1, waiting for transfers between devices: none -> 54.6 us  [on_device(): lax.all_gather(partial_value, ('space', 'tm'))]
    psum x1 -> x0, blocking collectives: 38.7 us -> none  [on_device(): gram_matrix = lax.psum(partial_value, ('space', 'tm'))]
  transfers between devices with their start and end apart: 2 -> 3, of which waited for: 2 -> 3; matrix products, arithmetic and copies ran while one was open for 0% -> 0% of each run, Pallas kernels for 0% -> 0%
where the time goes in v1:
time: 250 us
  waiting for transfers between devices  187 us (75%)
  other arithmetic  25.1 us (10%)
  matrix products  15.2 us (6%)
  between operations  14.8 us (6%)
  starting transfers between devices  6.16 us (2%)
    all_gather x1, waiting for transfers between devices, on_device(): lax.all_gather(coeffs, 'tm', axis=1, tiled=True)  126 us
    all_gather x1, waiting for transfers between devices, on_device(): lax.all_gather(partial_value, ('space', 'tm'))  54.6 us
    another operation x4, other arithmetic, on_device(): factor = jnp.linalg.cholesky(gram_matrix + ridge_term * identity[None])  11.9 us
    another operation x3, other arithmetic, on_device(): lax.linalg.triangular_solve(factor, columns, left_side=True, lower=True)  9.92 us
    dot_general x1, matrix products, on_device(): jnp.einsum('ct,htp->chp', second_table, halves, preferred_element_type=jn...  8.19 us
    ppermute x1, starting transfers between devices, passed_along(): lax.ppermute(array, axis, [(i, (i + by) % devices) for i in range(devices)])  6.09 us
    ppermute x1, waiting for transfers between devices, passed_along(): lax.ppermute(array, axis, [(i, (i + by) % devices) for i in range(devices)])  5.51 us
  transfers between devices with their start and end apart: 3, of which 3 were waited for; matrix products, arithmetic and copies ran while one was open for 0% of the time, Pallas kernels for 0%

profile of v1, /device:TPU:0, one launch (start us, length us, event | category | flops | bytes accessed | tf_op | source)
XLA Modules:
  0.0 250.0 jit_solution(6272371269823234661)
XLA Ops:
  7.2 0.0 all-gather.4.cloned.1.call-start
  7.2 0.6 multiply_reduce_fusion
  8.6 0.8 multiply_convert_fusion.1
  9.4 0.0 copy-start
  9.4 8.2 %fusion.8 = f32[4,4,16384]{2,0,1:T(4,128)S(1)} fusion(bf16[4,128,16384]{2,1,0:T(8,128)(2,1)} %bitcast.27, bf16[4,256]{1,0:T(4,128)(2,1)S(1)} %convert_element_type.35), kind=kOutput, calls=%fused_computation.25 | convolution fusion | flops 67108864 | bytes 17826816 | tf_op jit(solution)/shard_map/ct,htp->chp/dot_general | solution.py:36
  17.7 6.1 %collective-permute-start = (f32[4,1,16384]{2,0,1:T(4,128)S(1)}, f32[4,1,16384]{2,0,1:T(4,128)S(1)}, u32[]{:S(2)}, u32[]{:S(2)}) collective-permute-start(f32[4,1,16384]{2,0,1:T(4,128)S(1)} %slice.29), channel_id=1, source_target_pairs={{0,7},{1,0},{2,1},{3,2},{4,3},{5,4},{6,5},{7,6},{8,15},{9,8},{10,9... | collective-permute-start | bytes 786440 | tf_op jit(solution)/shard_map/ppermute | solution.py:14
  23.7 0.1 slice.28
  23.8 5.5 %collective-permute-done = f32[4,1,16384]{2,0,1:T(4,128)S(1)} collective-permute-done((f32[4,1,16384]{2,0,1:T(4,128)S(1)}, f32[4,1,16384]{2,0,1:T(4,128)S(1)}, u32[]{:S(2)}, u32[]{:S(2)}) %collective-permute-start) | collective-permute-done | bytes 262176 | tf_op jit(solution)/shard_map/ppermute | solution.py:14
  29.3 3.3 %maximum_add_fusion = f32[4,4,16384]{2,0,1:T(4,128)} fusion(f32[4,1,16384]{2,0,1:T(4,128)S(1)} %collective-permute-done, f32[4,3,16384]{2,0,1:T(4,128)S(1)} %slice.28, bf16[4,128,16384]{2,1,0:T(8,128)(2,1)S(1)} %bitcast.28, bf16[4,256]{1,0:T(4,128)(2,1)S(1)} %convert_element_type.35), kind=kOutput, calls=%fused_computation.1 | convolution fusion | flops 67633152 | bytes 18875392 | tf_op jit(solution)/shard_map/ct,htp->chp/dot_general | solution.py:35
  32.6 0.0 all-gather.4.cloned.1.call-update
  32.6 0.0 all-gather.6.cloned.1.call-start
  32.6 126.4 %all-gather.4.cloned.1.call-done = f32[4,32,16384]{2,0,1:T(4,128)} async-done(((f32[4,4,16384]{2,0,1:T(4,128)}), f32[4,32,16384]{2,0,1:T(4,128)}) %all-gather.4.cloned.1.call-update) | async-done | bytes 8388624 | tf_op jit(solution)/shard_map/all_gather | solution.py:43
  159.1 1.3 constant_dynamic-slice_fusion
  160.4 0.6 copy.27
  161.0 1.7 convolution_multiply_fusion
  162.7 0.0 all-gather.6.cloned.1.call-update
  162.8 54.6 %all-gather.6.cloned.1.call-done = f32[64,64,64]{2,1,0:T(8,128)} async-done(((f32[2,64,64]{2,1,0:T(8,128)}), f32[64,64,64]{2,1,0:T(8,128)}) %all-gather.6.cloned.1.call-update) | async-done | bytes 1048592 | tf_op jit(solution)/shard_map/all_gather | solution.py:51
  217.5 1.8 reduce_sum.21
  219.2 0.1 copy.24
  219.3 11.7 %custom-call.7 = f32[2,64,64]{2,1,0:T(8,128)S(1)} custom-call(f32[2,64,64]{2,1,0:T(8,128)S(1)} %fusion.3), custom_call_target="Cholesky" | custom-call | tf_op jit(solution)/shard_map/jit(cholesky)/cholesky | solution.py:53
  231.1 0.1 compare_reduce_fusion
  231.2 0.1 select_bitcast_fusion
  231.3 9.8 %custom-call.8 = f32[2,1,64,64]{2,3,1,0:T(8,128)S(1)} custom-call(f32[2,1,64,64]{3,2,1,0:T(8,128)S(1)} %select_bitcast_fusion), custom_call_target="InvertDiagBlocksLowerTriangular" | custom-call | tf_op jit(solution)/shard_map/triangular_solve | solution.py:54
  241.1 2.0 fusion
  (13 shorter events, 0.2 us)
Async XLA Ops:
  7.2 151.9 %all-gather.4.cloned.1.call-start = ((), (), s32[]{:S(2)}) async-start(), calls=%async_computation | async-start | bytes 9437184 | tf_op jit(solution)/shard_map/all_gather | solution.py:43
  9.4 19.9 %copy-start = (bf16[512,16384]{1,0:T(8,128)(2,1)S(1)}, bf16[512,16384]{1,0:T(8,128)(2,1)}, u32[]{:S(2)}) copy-start(bf16[512,16384]{1,0:T(8,128)(2,1)} %param.2) | copy-start | bytes 50331652
  17.7 11.7 %collective-permute-start = (f32[4,1,16384]{2,0,1:T(4,128)S(1)}, f32[4,1,16384]{2,0,1:T(4,128)S(1)}, u32[]{:S(2)}, u32[]{:S(2)}) collective-permute-start(f32[4,1,16384]{2,0,1:T(4,128)S(1)} %slice.29), channel_id=1, source_target_pairs={{0,7},{1,0},{2,1},{3,2},{4,3},{5,4},{6,5},{7,6},{8,15},{9,8},{10,9... | collective-permute-start | bytes 786440 | tf_op jit(solution)/shard_map/ppermute | solution.py:14
  32.6 184.9 %all-gather.6.cloned.1.call-start = ((), (), s32[]{:S(2)}) async-start(), calls=%async_computation.1 | async-start | bytes 2162688 | tf_op jit(solution)/shard_map/all_gather | solution.py:51
  219.2 23.9 %copy-start.1 = (f32[2,64,64]{2,1,0:T(8,128)}, f32[2,64,64]{2,1,0:T(8,128)S(1)}, u32[]{:S(2)}) copy-start(f32[2,64,64]{2,1,0:T(8,128)S(1)} %reduce_sum.21) | copy-start | bytes 98308
Sparse Core Ops, SparseCore 0:
  32.7 126.3 all-gather.3
  162.9 54.5 all-gather.5
